TPU v7x, 128 devices: a whole 4x4x4 slice. The times are simulated.
128 devices in a mesh: slab: 32 (over y, z, x_lo), beam: 4 (over x_hi, core).
Axes of the slice: x: 4 (x_hi: 2, x_lo: 2; x = x_hi * 2 + x_lo), y: 4, z: 4, core: 2. Of those that a mesh axis runs over, the one named last changes fastest.
Arguments:
- traces: bfloat16 [2048, 128, 1024], P(('slab', 'beam')), may hold values from -6 to 6
- shot_window: int32 [2048], P(('slab', 'beam')), may hold values from 0 to 15, as said below
- trace_slot: int32 [2048, 128], P(('slab', 'beam')), may hold values from 0 to 63
- ray_phase: bfloat16 [256, 1024], replicated, may hold values from -0.1875 to 0.1875
- ray_index: int32 [16, 768], P('beam', 'slab'), may hold values from 0 to 255
- beam_basis: bfloat16 [2, 1024, 8192], P(None, 'beam'), may hold values from -0.125 to 0.125
Outputs:
- image: float32 [768, 8192], P('slab', 'beam')
Inputs may be any that keep to these rules, and one draw needn't show every extreme that they name: `shot_window`: within each aligned block of 16 shots (the shots of one device), for every beam owner b exactly 4 shots name a window w with w // 4 = b.
All inputs are finite; a program needn't handle non-finite values.
Results may differ from a plain program's by a relative error of at most 0.0041.
Values may be sent and summed in bfloat16 or wider, within the bound.
No kernel may reach another device: no remote copies, remote signals or barrier semaphores. Data moves between devices by JAX's collectives and lax.ppermute only.
A program may use at most 64 MiB of HBM per device.

v0:
```python
import math
import jax
import jax.numpy as jnp
from jax import lax
from jax.sharding import PartitionSpec as P

P_SIZE = 64
K = 64
WIN_OWN = 4


def slant_tables():
    phase_steps = (
        jnp.arange(P_SIZE, dtype=jnp.int32)[:, None] * jnp.arange(K, dtype=jnp.int32)[None, :] % K
    )
    angles = phase_steps.astype(jnp.float32) * jnp.float32(2.0 * math.pi / K)
    return (jnp.cos(angles), jnp.sin(angles))


def slant_stack(binned, cosine_table, sine_table):
    freq_count = binned.shape[-1] // 2
    real_part = binned[..., :freq_count]
    imag_part = binned[..., freq_count:]
    high = lax.Precision.HIGHEST
    panel_re = jnp.einsum("ps,wsf->wpf", cosine_table, real_part, precision=high) + jnp.einsum(
        "ps,wsf->wpf", sine_table, imag_part, precision=high
    )
    panel_im = jnp.einsum("ps,wsf->wpf", cosine_table, imag_part, precision=high) - jnp.einsum(
        "ps,wsf->wpf", sine_table, real_part, precision=high
    )
    return jnp.concatenate([panel_re, panel_im], axis=-1)


def bin_traces(samples, labels, wanted):
    binning = (wanted[:, None] == labels[None, :]).astype(jnp.bfloat16)
    return jnp.dot(binning, samples, preferred_element_type=jnp.float32)


def body(traces, shot_window, trace_slot, ray_phase, ray_index, beam_basis):
    shot_count, per_shot, doubled = traces.shape
    freq_count = doubled // 2
    beam_count = lax.axis_size("beam")
    slab_count = lax.axis_size("slab")
    stack_scale = (shot_count * slab_count * beam_count * per_shot / (WIN_OWN * beam_count)) ** (
        -0.5
    )
    cosine_table, sine_table = slant_tables()
    owners = shot_window // WIN_OWN
    matches = (owners[:, None] == jnp.arange(beam_count, dtype=jnp.int32)[None, :]).astype(
        jnp.int32
    )
    rank_in = jnp.sum(jnp.cumsum(matches, axis=0) * matches, axis=1) - 1
    target = owners * (shot_count // beam_count) + rank_in
    gather_order = (
        jnp.zeros((shot_count,), jnp.int32).at[target].set(jnp.arange(shot_count, dtype=jnp.int32))
    )
    local_labels = ((shot_window % WIN_OWN)[:, None] * K + trace_slot).astype(jnp.bfloat16)
    arrived, arrived_labels = (
        lax.all_to_all(traces[gather_order], "beam", split_axis=0, concat_axis=0, tiled=True),
        lax.all_to_all(local_labels[gather_order], "beam", split_axis=0, concat_axis=0, tiled=True),
    )
    labels = arrived_labels.astype(jnp.int32).reshape(-1)
    samples = arrived.reshape(-1, doubled)
    binned = bin_traces(samples, labels, jnp.arange(WIN_OWN * K, dtype=jnp.int32))
    partial_value = slant_stack(binned.reshape(WIN_OWN, K, doubled), cosine_table, sine_table)
    partial_value = partial_value.reshape(WIN_OWN * P_SIZE, doubled) * jnp.float32(stack_scale)
    beam_panel = lax.psum(partial_value, "slab").astype(jnp.bfloat16)
    ray_count = ray_phase.shape[0]
    depths = ray_index.shape[1]
    ray_pick = (
        ray_index.reshape(-1)[:, None] == jnp.arange(ray_count, dtype=jnp.int32)[None, :]
    ).astype(jnp.bfloat16)
    rays = jnp.dot(ray_pick, ray_phase, preferred_element_type=jnp.float32).astype(jnp.bfloat16)
    rays = rays.reshape(WIN_OWN, depths, doubled)
    panel_three = beam_panel.reshape(WIN_OWN, P_SIZE, doubled)
    panel_re = panel_three[..., :freq_count]
    panel_im = panel_three[..., freq_count:]
    left_re = jnp.concatenate([panel_re, -panel_im], axis=-1)
    left_im = jnp.concatenate([panel_im, panel_re], axis=-1)
    wave_re = jnp.einsum("wzf,wpf->zwp", rays, left_re, preferred_element_type=jnp.float32).astype(
        jnp.bfloat16
    )
    wave_im = jnp.einsum("wzf,wpf->zwp", rays, left_im, preferred_element_type=jnp.float32).astype(
        jnp.bfloat16
    )
    mixture = jnp.concatenate(
        [wave_re.reshape(depths, WIN_OWN * P_SIZE), -wave_im.reshape(depths, WIN_OWN * P_SIZE)],
        axis=1,
    )
    basis_rows = beam_basis.reshape(2 * WIN_OWN * P_SIZE, beam_basis.shape[2])
    image_part = jnp.dot(mixture, basis_rows, preferred_element_type=jnp.float32)
    return lax.psum_scatter(image_part, "beam", scatter_dimension=1, tiled=True)


def solution(mesh):
    in_specs = (
        P(("slab", "beam"), None, None),
        P(("slab", "beam")),
        P(("slab", "beam"), None),
        P(),
        P("beam", "slab"),
        P(None, "beam", None),
    )
    out_specs = P("slab", "beam")
    return jax.shard_map(body, mesh=mesh, in_specs=in_specs, out_specs=out_specs, check_vma=False)
```

profile of v0, /device:TPU:1, one launch (start us, length us, event | category | flops | bytes accessed | tf_op | source)
XLA Modules:
  0.0 295.8 jit_solution(17968223047291159660)
XLA Ops:
  6.5 0.0 copy-start
  6.5 0.7 fusion.43
  7.3 0.1 fusion.42
  7.4 0.2 select_reduce_fusion
  7.6 0.6 scatter_custom_fusion
  8.2 0.8 add_convert_fusion
  9.0 1.2 gather_fusion
  10.2 5.8 %all-to-all-start = ((bf16[4,4,128]{2,1,0:T(4,128)(2,1)}), bf16[4,4,128]{2,1,0:T(4,128)(2,1)S(1)}, u32[]{:S(2)}, u32[]{:S(2)}) async-start(bf16[4,4,128]{2,1,0:T(4,128)(2,1)} %bitcast), calls=%async_computation | async-start | bytes 8192 | tf_op jit(solution)/shard_map/all_to_all | solution.py:60
  15.9 5.0 %gather_fusion.1 = bf16[16,128,1024]{2,1,0:T(8,128)(2,1)} fusion(bf16[16,128,1024]{2,1,0:T(8,128)(2,1)} %param.6, s32[1024]{0:T(1024)S(1)} %pad_clamp_fusion), kind=kCustom, calls=%fused_computation.1 | custom fusion | bytes 8388672 | tf_op jit(solution)/shard_map/gather | solution.py:59
  20.9 0.0 all-to-all-done
  20.9 5.1 %all-to-all-start.1 = ((bf16[16,128,1024]{2,1,0:T(8,128)(2,1)}), bf16[16,128,1024]{2,1,0:T(8,128)(2,1)}, u32[]{:S(2)}, u32[]{:S(2)}) async-start(bf16[16,128,1024]{2,1,0:T(8,128)(2,1)} %gather_fusion.1), calls=%async_computation.1 | async-start | bytes 8388608 | tf_op jit(solution)/shard_map/all_to_all | solution.py:59
  26.1 0.0 reduce-scatter.2.cloned.1.call-start
  26.1 0.0 copy-done.1
  26.1 0.1 eq.65
  26.2 0.0 copy-done
  26.2 0.3 convolution_convert_fusion
  26.4 48.4 %all-to-all-done.1 = bf16[16,128,1024]{2,1,0:T(8,128)(2,1)} async-done(((bf16[16,128,1024]{2,1,0:T(8,128)(2,1)}), bf16[16,128,1024]{2,1,0:T(8,128)(2,1)}, u32[]{:S(2)}, u32[]{:S(2)}) %all-to-all-start.1) | async-done | bytes 4194336 | tf_op jit(solution)/shard_map/all_to_all | solution.py:59
  74.8 3.5 %fusion = f32[4,64,1024]{2,1,0:T(8,128)S(1)} fusion(bf16[2048,1024,1]{1,0,2:T(8,128)(2,1)} %bitcast.3, s32[2048]{0:T(1024)S(1)} %convert.1, s32[4,64]{1,0:T(4,128)S(1)} %multiply_add_fusion), kind=kOutput, calls=%fused_computation.3 | convolution fusion | flops 1074266112 | bytes 5252096 | tf_op jit(solution)/shard_map/dot_general | solution.py:36
  78.3 0.8 fusion.19
  79.1 0.8 fusion.15
  79.9 0.8 fusion.3
  80.6 0.8 fusion.2
  81.4 0.1 maximum_multiply_fusion
  81.5 149.0 %all-reduce.1 = bf16[256,1024]{1,0:T(8,128)(2,1)S(1)} all-reduce(f32[256,1024]{1,0:T(8,128)S(1)} %bitcast.34), channel_id=1, replica_groups=mesh['slab'=32,'beam'=4] {'slab'}, use_global_device_ids=true, to_apply=%region_3.4 | all-reduce | flops 262144 | bytes 1572864 | tf_op jit(solution)/shard_map/psum | solution.py:67
  230.5 0.1 slice_negate_fusion
  230.6 0.2 fusion.4
  230.8 0.1 reshape.55
  230.9 0.2 fusion.6
  231.2 0.1 neg.15
  231.3 5.5 %fusion.32 = f32[24,8192]{1,0:T(8,128)} fusion(bf16[512,8192]{1,0:T(8,128)(2,1)} %bitcast.33, bf16[24,256]{1,0:T(8,128)(2,1)S(1)} %neg.15, bf16[24,256]{1,0:T(8,128)(2,1)S(1)} %reshape.55), kind=kOutput, calls=%fused_computation.45 | convolution fusion | flops 201375744 | bytes 9199616 | tf_op jit(solution)/shard_map/dot_general | solution.py:91
  236.8 0.0 reduce-scatter.2.cloned.1.call-update
  236.8 52.1 %reduce-scatter.2.cloned.1.call-done = f32[24,2048]{1,0:T(8,128)} async-done(((f32[24,8192]{1,0:T(8,128)}), f32[24,2048]{1,0:T(8,128)}) %reduce-scatter.2.cloned.1.call-update) | async-done | bytes 196624 | tf_op jit(solution)/shard_map/reduce_scatter | solution.py:92
  (10 shorter events, 0.1 us)
Async XLA Ops:
  6.5 19.6 %copy-start = (bf16[256,1024]{1,0:T(8,128)(2,1)S(1)}, bf16[256,1024]{1,0:T(8,128)(2,1)}, u32[]{:S(2)}) copy-start(bf16[256,1024]{1,0:T(8,128)(2,1)} %param.9) | copy-start | bytes 1572868
  10.2 10.8 %all-to-all-start = ((bf16[4,4,128]{2,1,0:T(4,128)(2,1)}), bf16[4,4,128]{2,1,0:T(4,128)(2,1)S(1)}, u32[]{:S(2)}, u32[]{:S(2)}) async-start(bf16[4,4,128]{2,1,0:T(4,128)(2,1)} %bitcast), calls=%async_computation | async-start | bytes 8192 | tf_op jit(solution)/shard_map/all_to_all | solution.py:60
  20.9 5.1 %copy-start.1 = (s32[4,24]{1,0:T(4,128)S(1)}, s32[4,24]{1,0:T(4,128)}, u32[]{:S(2)}) copy-start(s32[4,24]{1,0:T(4,128)} %param.10) | copy-start | bytes 1156
  20.9 53.9 %all-to-all-start.1 = ((bf16[16,128,1024]{2,1,0:T(8,128)(2,1)}), bf16[16,128,1024]{2,1,0:T(8,128)(2,1)}, u32[]{:S(2)}, u32[]{:S(2)}) async-start(bf16[16,128,1024]{2,1,0:T(8,128)(2,1)} %gather_fusion.1), calls=%async_computation.1 | async-start | bytes 8388608 | tf_op jit(solution)/shard_map/all_to_all | solution.py:59
  26.1 262.9 %reduce-scatter.2.cloned.1.call-start = ((), (), s32[]{:S(2)}) async-start(), calls=%async_computation.3 | async-start | bytes 983040 | tf_op jit(solution)/shard_map/reduce_scatter | solution.py:92
Sparse Core Ops, SparseCore 0:
  236.9 51.9 reduce-scatter.1
where the time goes:
time: 296 us
  blocking collectives  149 us (50%)
  waiting for transfers between devices  101 us (34%)
  between operations  13.5 us (5%)
  matrix products  12.8 us (4%)
  starting transfers between devices  10.9 us (4%)
  local copies, waits for them, and re-layouts  7.07 us (2%)
    psum x1, blocking collectives, body(): beam_panel = lax.psum(partial_value, 'slab').astype(jnp.bfloat16)  149 us
    reduce_scatter x1, waiting for transfers between devices, body(): return lax.psum_scatter(image_part, 'beam', scatter_dimension=1, tiled=True)  52.1 us
    all_to_all x1, waiting for transfers between devices, body(): lax.all_to_all(traces[gather_order], 'beam', split_axis=0, concat_axis=0,...  48.4 us
  transfers between devices with their start and end apart: 3, of which 2 were waited for; matrix products, arithmetic and copies ran while one was open for 2% of the time, Pallas kernels for 0%

commit v1 on v0

--- a/solution.py
+++ b/solution.py
@@ -64,7 +64,7 @@
     binned = bin_traces(samples, labels, jnp.arange(WIN_OWN * K, dtype=jnp.int32))
     partial_value = slant_stack(binned.reshape(WIN_OWN, K, doubled), cosine_table, sine_table)
     partial_value = partial_value.reshape(WIN_OWN * P_SIZE, doubled) * jnp.float32(stack_scale)
-    beam_panel = lax.psum(partial_value, "slab").astype(jnp.bfloat16)
+    beam_panel = jnp.sum(lax.all_gather(partial_value, "slab"), axis=0).astype(jnp.bfloat16)
     ray_count = ray_phase.shape[0]
     depths = ray_index.shape[1]
     ray_pick = (

time: 296 us -> 848 us (2.86)
  waiting for transfers between devices: 101 us -> 789 us
  blocking collectives: 149 us -> 0 us
  other arithmetic: 1.96 us -> 14.8 us
    all_gather x0 -> x1, waiting for transfers between devices: none -> 710 us  [body(): lax.all_gather(partial_value, 'slab')]
    psum x1 -> x0, blocking collectives: 149 us -> none  [body(): beam_panel = lax.psum(partial_value, 'slab').astype(jnp.bfloat16)]
    reduce_scatter x1, waiting for transfers between devices: 52.1 us -> 29.5 us  [body(): return lax.psum_scatter(image_part, 'beam', scatter_dimension=1, tiled=True)]
    reduce_sum x0 -> x1, other arithmetic: none -> 11.9 us  [body(): jnp.sum(lax.all_gather(partial_value, 'slab'), axis=0).astype(jnp.bfloat16)]
  transfers between devices with their start and end apart: 3 -> 4, of which waited for: 2 -> 3; matrix products, arithmetic and copies ran while one was open for 2% -> 1% of each run, Pallas kernels for 0% -> 0%
where the time goes in v1:
time: 848 us
  waiting for transfers between devices  789 us (93%)
  other arithmetic  14.8 us (2%)
  between operations  13.5 us (2%)
  matrix products  12.8 us (2%)
  starting transfers between devices  11 us (1%)
    all_gather x1, waiting for transfers between devices, body(): lax.all_gather(partial_value, 'slab')  710 us
    all_to_all x1, waiting for transfers between devices, body(): lax.all_to_all(traces[gather_order], 'beam', split_axis=0, concat_axis=0,...  48.8 us
    reduce_scatter x1, waiting for transfers between devices, body(): return lax.psum_scatter(image_part, 'beam', scatter_dimension=1, tiled=True)  29.5 us
  transfers between devices with their start and end apart: 4, of which 3 were waited for; matrix products, arithmetic and copies ran while one was open for 1% of the time, Pallas kernels for 0%

profile of v1, /device:TPU:1, one launch (start us, length us, event | category | flops | bytes accessed | tf_op | source)
XLA Modules:
  0.0 847.7 jit_solution(53404758039857856)
XLA Ops:
  6.5 0.7 fusion.43
  7.3 0.1 fusion.42
  7.4 0.2 select_reduce_fusion
  7.6 0.6 scatter_custom_fusion
  8.2 0.8 add_convert_fusion
  9.0 1.2 gather_fusion
  10.2 5.8 all-to-all-start
  15.9 5.0 gather_fusion.1
  20.9 0.0 all-to-all-done
  20.9 5.1 all-to-all-start.1
  26.1 48.8 %all-to-all-done.1 = bf16[16,128,1024]{2,1,0:T(8,128)(2,1)} async-done(((bf16[16,128,1024]{2,1,0:T(8,128)(2,1)}), bf16[16,128,1024]{2,1,0:T(8,128)(2,1)}, u32[]{:S(2)}, u32[]{:S(2)}) %all-to-all-start.1) | async-done | bytes 4194336 | tf_op jit(solution)/shard_map/all_to_all | solution.py:59
  74.8 3.5 fusion
  78.3 0.0 copy-start.1
  78.3 0.8 fusion.19
  79.1 0.8 fusion.15
  79.9 0.8 fusion.3
  80.6 0.8 fusion.2
  81.4 1.1 maximum_multiply_fusion
  82.5 0.0 all-gather.2.cloned.1.call-update
  82.5 0.0 reduce-scatter.2.cloned.1.call-start
  82.6 0.1 eq.65
  82.7 0.3 convolution_convert_fusion
  82.9 710.2 %all-gather.2.cloned.1.call-done = f32[32,256,1024]{2,1,0:T(8,128)} async-done(((f32[1,256,1024]{2,1,0:T(8,128)}), f32[32,256,1024]{2,1,0:T(8,128)}) %all-gather.2.cloned.1.call-update) | async-done | bytes 33554448 | tf_op jit(solution)/shard_map/all_gather | solution.py:67
  793.1 11.9 %reduce_sum.19 = bf16[256,1024]{1,0:T(8,128)(2,1)S(1)} reduce(f32[32,256,1024]{2,1,0:T(8,128)} %all-gather.2.cloned.1.call-done, f32[]{:T(128)} %constant.60.clone.1), dimensions={0}, to_apply=%region_3.4 | reduce | flops 8126464 | bytes 34078724 | tf_op jit(solution)/shard_map/reduce_sum | solution.py:67
  805.0 0.1 slice_negate_fusion
  805.1 0.2 fusion.4
  805.4 0.1 reshape.64
  805.5 0.2 fusion.6
  805.8 0.1 neg.15
  805.8 5.5 fusion.32
  811.3 0.0 reduce-scatter.2.cloned.1.call-update
  811.4 29.5 %reduce-scatter.2.cloned.1.call-done = f32[24,2048]{1,0:T(8,128)} async-done(((f32[24,8192]{1,0:T(8,128)}), f32[24,2048]{1,0:T(8,128)}) %reduce-scatter.2.cloned.1.call-update) | async-done | bytes 196624 | tf_op jit(solution)/shard_map/reduce_scatter | solution.py:92
  (13 shorter events, 0.1 us)
Async XLA Ops:
  6.5 76.2 %copy-start = (bf16[256,1024]{1,0:T(8,128)(2,1)S(1)}, bf16[256,1024]{1,0:T(8,128)(2,1)}, u32[]{:S(2)}) copy-start(bf16[256,1024]{1,0:T(8,128)(2,1)} %param.9) | copy-start | bytes 1572868
  10.2 10.8 %all-to-all-start = ((bf16[4,4,128]{2,1,0:T(4,128)(2,1)}), bf16[4,4,128]{2,1,0:T(4,128)(2,1)S(1)}, u32[]{:S(2)}, u32[]{:S(2)}) async-start(bf16[4,4,128]{2,1,0:T(4,128)(2,1)} %bitcast), calls=%async_computation | async-start | bytes 8192 | tf_op jit(solution)/shard_map/all_to_all | solution.py:60
  20.9 53.9 %all-to-all-start.1 = ((bf16[16,128,1024]{2,1,0:T(8,128)(2,1)}), bf16[16,128,1024]{2,1,0:T(8,128)(2,1)}, u32[]{:S(2)}, u32[]{:S(2)}) async-start(bf16[16,128,1024]{2,1,0:T(8,128)(2,1)} %gather_fusion.1), calls=%async_computation.1 | async-start | bytes 8388608 | tf_op jit(solution)/shard_map/all_to_all | solution.py:59
  26.1 767.1 %all-gather.2.cloned.1.call-start = ((), (), s32[]{:S(2)}) async-start(), calls=%async_computation.3 | async-start | bytes 34603008 | tf_op jit(solution)/shard_map/all_gather | solution.py:67
  78.3 4.3 copy-start.1
  82.5 758.4 %reduce-scatter.2.cloned.1.call-start = ((), (), s32[]{:S(2)}) async-start(), calls=%async_computation.4 | async-start | bytes 983040 | tf_op jit(solution)/shard_map/reduce_scatter | solution.py:92
Sparse Core Ops, SparseCore 0:
  82.7 710.4 all-gather.1
  811.5 29.3 reduce-scatter.1
